TPU v7x, 512 devices: a whole 4x8x8 slice. The times are simulated.
512 devices in a mesh: grp: 16 (over y, core), ops: 32 (over x, z).
Axes of the slice: x: 4, y: 8, z: 8, core: 2. Of those that a mesh axis runs over, the one named last changes fastest.
Arguments:
- op_embed: bfloat16 [131072, 256], P(('grp', 'ops')), may hold values from -6 to 6
- machine_embed: bfloat16 [8192, 256], P('grp'), may hold values from -6 to 6
- cotangent: bfloat16 [131072, 256], P(('grp', 'ops')), may hold values from -6 to 6
- w_query: bfloat16 [256, 256], replicated, may hold values from -0.375 to 0.375
- w_key: bfloat16 [256, 256], replicated, may hold values from -0.375 to 0.375
- w_value: bfloat16 [256, 256], replicated, may hold values from -0.375 to 0.375
- slot_local: int32 [512, 16], P(('grp', 'ops')), may hold values from 0 to 3
- counts: int32 [131072, 16], P(('grp', 'ops')), may hold values from 0 to 128, as said below
Outputs:
- op_grad: bfloat16 [131072, 256], P(('grp', 'ops'))
- machine_grad: float32 [8192, 256], P(('grp', 'ops'))
- grad_wq: float32 [256, 256], replicated
- grad_wk: float32 [256, 256], replicated
- grad_wv: float32 [256, 256], replicated
Inputs may be any that keep to these rules, and one draw needn't show every extreme that they name: The eligible machines of slot e's block for operation o are its first counts[o, e] machines; 0 means the operation has no eligible machine in that block.
All inputs are finite; a program needn't handle non-finite values.
Results may differ from a plain program's by a relative error of at most 0.0056.
Values may be sent and summed in bfloat16 or wider, within the bound.
No kernel may reach another device: no remote copies, remote signals or barrier semaphores. Data moves between devices by JAX's collectives and lax.ppermute only.
A program may use at most 64 MiB of HBM per device.

v0:
```python
import jax
import jax.numpy as jnp
from jax import lax
from jax.sharding import PartitionSpec as P

HEADS = 8
BLK = 128
mean_scale = 0.08838834764831845


def slot_grads(queries, cotangent4, key_rows, value_rows, lengths):
    head_size = queries.shape[2]
    inv_root = head_size ** (-0.5)
    scores = (
        jnp.einsum("ohc,mhc->ohm", queries, key_rows, preferred_element_type=jnp.float32) * inv_root
    )
    sigmoid_score = jax.nn.sigmoid(scores)
    columns = lax.broadcasted_iota(jnp.int32, scores.shape, 2)
    eligible = columns < lengths[:, None, None]
    gates = jnp.where(eligible, sigmoid_score, 0.0).astype(jnp.bfloat16)
    value_dot = jnp.einsum(
        "ohc,mhc->ohm", cotangent4, value_rows, preferred_element_type=jnp.float32
    )
    dscore = jnp.where(
        eligible, mean_scale * value_dot * sigmoid_score * (1.0 - sigmoid_score) * inv_root, 0.0
    ).astype(jnp.bfloat16)
    query_part = jnp.einsum("ohm,mhc->ohc", dscore, key_rows, preferred_element_type=jnp.float32)
    key_grad = jnp.einsum(
        "ohm,ohc->mhc", dscore, queries, preferred_element_type=jnp.float32
    ).astype(jnp.bfloat16)
    value_grad = (
        mean_scale
        * jnp.einsum("ohm,ohc->mhc", gates, cotangent4, preferred_element_type=jnp.float32)
    ).astype(jnp.bfloat16)
    return (query_part, key_grad, value_grad)


def per_device(op_embed, machine_embed, cotangent, w_query, w_key, w_value, slot_local, counts):
    groups = lax.axis_size("grp")
    ops_count = op_embed.shape[0]
    model_width = op_embed.shape[1]
    head_size = model_width // HEADS
    machine_rows = machine_embed.shape[0]
    blocks_here = machine_rows // BLK
    highest = lax.Precision.HIGHEST
    both_weights = jnp.concatenate([w_key, w_value], axis=1)
    queries = jnp.dot(op_embed, w_query, preferred_element_type=jnp.float32).astype(jnp.bfloat16)
    wanted = lax.all_to_all(
        slot_local.reshape(groups, 1), "grp", split_axis=0, concat_axis=0, tiled=True
    )
    wanted_ids = wanted[:, 0]
    picker = wanted_ids[:, None] == jnp.arange(blocks_here, dtype=jnp.int32)[None, :]
    local_pairs = jnp.dot(machine_embed, both_weights, preferred_element_type=jnp.float32).astype(
        jnp.bfloat16
    )
    outgoing = local_pairs.reshape(blocks_here, BLK, 2 * model_width)[wanted_ids]
    fetched = lax.all_to_all(outgoing, "grp", split_axis=0, concat_axis=0, tiled=True)
    key_slots = fetched[:, :, :model_width].reshape(groups, BLK, HEADS, head_size)
    value_slots = fetched[:, :, model_width:].reshape(groups, BLK, HEADS, head_size)
    query_heads = queries.reshape(ops_count, HEADS, head_size)
    cot_heads = cotangent.reshape(ops_count, HEADS, head_size)

    def per_slot(summed_q, pieces):
        key_rows, value_rows, lengths = pieces
        query_part, key_grad, value_grad = slot_grads(
            query_heads, cot_heads, key_rows, value_rows, lengths
        )
        return (
            summed_q + query_part,
            (key_grad.reshape(BLK, model_width), value_grad.reshape(BLK, model_width)),
        )

    start_q = jnp.zeros((ops_count, HEADS, head_size), jnp.float32)
    summed_q, (key_grads, value_grads) = lax.scan(
        per_slot, start_q, (key_slots, value_slots, counts.T)
    )
    grad_query = summed_q.astype(jnp.bfloat16).reshape(ops_count, model_width)
    op_grad = (
        cotangent.astype(jnp.float32)
        + jnp.dot(grad_query, w_query.T, preferred_element_type=jnp.float32)
    ).astype(jnp.bfloat16)
    wq_term = jnp.einsum("od,oe->de", op_embed, grad_query, preferred_element_type=jnp.float32)
    returned = lax.all_to_all(
        jnp.concatenate([key_grads, value_grads], axis=2),
        "grp",
        split_axis=0,
        concat_axis=0,
        tiled=True,
    )
    summed = jnp.einsum(
        "gb,gr->br",
        picker.astype(jnp.bfloat16),
        returned.reshape(groups, BLK * 2 * model_width),
        preferred_element_type=jnp.float32,
    )
    summed = summed.reshape(machine_rows, 2 * model_width)
    key_total = summed[:, :model_width]
    value_total = summed[:, model_width:]
    machine_part = jnp.dot(key_total, w_key.astype(jnp.float32).T, precision=highest) + jnp.dot(
        value_total, w_value.astype(jnp.float32).T, precision=highest
    )
    embed_f = machine_embed.astype(jnp.float32)
    wk_term = jnp.dot(embed_f.T, key_total, precision=highest)
    wv_term = jnp.dot(embed_f.T, value_total, precision=highest)
    summed_total = lax.psum(machine_part, "ops")
    share_rows = machine_rows // lax.axis_size("ops")
    first_row = lax.axis_index("ops") * share_rows
    machine_grad = lax.dynamic_slice_in_dim(summed_total, first_row, share_rows, 0)
    weight_sums = lax.psum((wq_term, wk_term, wv_term), ("grp", "ops"))
    shard_count = float(groups * lax.axis_size("ops"))
    grad_wq = weight_sums[0] / shard_count
    grad_wk = weight_sums[1] / shard_count
    grad_wv = weight_sums[2] / shard_count
    return (op_grad, machine_grad, grad_wq, grad_wk, grad_wv)


def solution(mesh):
    return jax.shard_map(
        per_device,
        mesh=mesh,
        in_specs=(
            P(("grp", "ops"), None),
            P("grp", None),
            P(("grp", "ops"), None),
            P(),
            P(),
            P(),
            P(("grp", "ops"), None),
            P(("grp", "ops"), None),
        ),
        out_specs=(P(("grp", "ops"), None), P(("grp", "ops"), None), P(), P(), P()),
        check_vma=False,
    )
```

profile of v0, /device:TPU:8, one launch (start us, length us, event | category | flops | bytes accessed | tf_op | source)
XLA Modules:
  0.0 657.2 jit_solution(9235457132968034616)
XLA Ops:
  7.2 1.4 copy.46
  8.6 9.1 %all-to-all-start = ((s32[16,1,1]{2,1,0:T(1,128)}), s32[16,1,1]{2,1,0:T(1,128)S(1)}, u32[]{:S(2)}, u32[]{:S(2)}) async-start(s32[16,1,1]{2,1,0:T(1,128)} %copy.46), calls=%async_computation | async-start | bytes 16384 | tf_op jit(solution)/shard_map/all_to_all | solution.py:48
  17.6 1.3 convolution_convert_fusion.1
  18.9 4.9 all-to-all-done
  24.2 2.0 gather_fusion
  26.2 5.1 all-to-all-start.1
  31.7 46.8 %all-to-all-done.1 = bf16[16,128,512]{2,1,0:T(8,128)(2,1)S(1)} async-done(((bf16[16,128,512]{2,1,0:T(8,128)(2,1)}), bf16[16,128,512]{2,1,0:T(8,128)(2,1)S(1)}, u32[]{:S(2)}, u32[]{:S(2)}) %all-to-all-start.1) | async-done | bytes 2097184 | tf_op jit(solution)/shard_map/all_to_all | solution.py:57
  78.6 1.6 fusion.38
  80.2 1.7 copy.47
  81.9 1.3 copy.48
  83.2 63.6 %while.15 = (s32[]{:T(128)}, f32[256,8,32]{0,2,1:T(8,128)S(1)}, bf16[16,128,256]{1,2,0:T(8,128)(2,1)}, bf16[16,128,256]{1,2,0:T(8,128)(2,1)}, bf16[16,128,8,32]{...) while((s32[]{:T(128)}, f32[256,8,32]{0,2,1:T(8,128)S(1)}, ...), condition=%wide.region_1.2_spmd.clone, body=%wide.region_0.1_spmd.clone.sunk | while | flops 87785472 | bytes 6361235 | solution.py:74
  83.7 0.7 constant_dynamic-slice_fusion.3
  84.4 1.3 fusion.80
  86.5 0.7 bitcast_dynamic-update-slice_fusion.3
  87.7 0.7 constant_dynamic-slice_fusion.3
  88.4 1.3 fusion.80
  91.7 0.7 constant_dynamic-slice_fusion.3
  92.4 1.3 fusion.80
  95.6 0.7 constant_dynamic-slice_fusion.3
  96.3 1.3 fusion.80
  99.6 0.7 constant_dynamic-slice_fusion.3
  100.3 1.3 fusion.80
  103.6 0.7 constant_dynamic-slice_fusion.3
  104.3 1.3 fusion.80
  107.5 0.7 constant_dynamic-slice_fusion.3
  108.2 1.3 fusion.80
  110.3 0.7 bitcast_dynamic-update-slice_fusion.3
  111.5 0.7 constant_dynamic-slice_fusion.3
  112.2 1.3 fusion.80
  115.5 0.7 constant_dynamic-slice_fusion.3
  116.2 1.3 fusion.80
  119.5 0.7 constant_dynamic-slice_fusion.3
  120.2 1.3 fusion.80
  123.4 0.7 constant_dynamic-slice_fusion.3
  124.1 1.3 fusion.80
  127.4 0.7 constant_dynamic-slice_fusion.3
  128.1 1.3 fusion.80
  130.2 0.7 bitcast_dynamic-update-slice_fusion.3
  131.4 0.7 constant_dynamic-slice_fusion.3
  132.1 1.3 fusion.80
  135.4 0.7 constant_dynamic-slice_fusion.3
  136.1 1.3 fusion.80
  139.3 0.7 constant_dynamic-slice_fusion.3
  140.1 1.3 fusion.80
  143.3 0.7 constant_dynamic-slice_fusion.3
  144.0 1.3 fusion.80
  146.8 3.1 pad_maximum_fusion
  149.9 6.9 %all-to-all-start.2 = ((bf16[16,128,512]{1,2,0:T(8,128)(2,1)}), bf16[16,128,512]{1,2,0:T(8,128)(2,1)}, u32[]{:S(2)}, u32[]{:S(2)}) async-start(bf16[16,128,512]{1,2,0:T(8,128)(2,1)} %pad_maximum_fusion), calls=%async_computation.2 | async-start | bytes 4194304 | tf_op jit(solution)/shard_map/all_to_all | solution.py:83
  156.8 0.9 convolution_bitcast_fusion.3
  157.7 46.3 %all-to-all-done.2 = bf16[16,128,512]{1,2,0:T(8,128)(2,1)} async-done(((bf16[16,128,512]{1,2,0:T(8,128)(2,1)}), bf16[16,128,512]{1,2,0:T(8,128)(2,1)}, u32[]{:S(2)}, u32[]{:S(2)}) %all-to-all-start.2) | async-done | bytes 2097184 | tf_op jit(solution)/shard_map/all_to_all | solution.py:83
  204.0 3.4 copy.57
  208.0 0.7 reshape.79
  208.7 1.3 convolution_bitcast_fusion.2
  210.0 1.3 convolution_bitcast_fusion.1
  211.9 1.2 convolution_add_fusion
  213.1 0.9 fusion.25
  214.0 274.6 %all-reduce.6.cloned.1.call-done = (f32[256,256]{0,1:T(8,128)}, f32[256,256]{0,1:T(8,128)}, f32[256,256]{0,1:T(8,128)}) async-done(((f32[256,256]{0,1:T(8,128)}, f32[256,256]{0,1:T(8,128)}, f32[256,256]{0,1:T(8,128)}), (f32[256,256]{0,1:T(8,128)}, f32[256,256]{0,1:T(8,128)}, f32[256,256]{0,1:T(8,128)})) %all-reduce.6.cloned.1.call-update) | async-done | bytes 786448 | tf_op jit(solution)/shard_map/psum | solution.py:109
  488.6 1.0 broadcast_multiply_fusion.2
  489.6 0.8 copy.51
  490.4 1.1 broadcast_multiply_fusion
  491.5 0.8 copy.52
  492.3 0.8 copy.53
  493.2 155.8 %all-reduce.4.cloned.1.call-done = f32[512,256]{1,0:T(8,128)} async-done(((f32[512,256]{1,0:T(8,128)}), f32[512,256]{1,0:T(8,128)}) %all-reduce.4.cloned.1.call-update) | async-done | bytes 524304 | tf_op jit(solution)/shard_map/psum | solution.py:105
  649.0 1.3 constant_dynamic-slice_fusion.1
  (112 shorter events, 30.7 us)
Async XLA Ops:
  7.2 10.5 %copy-start = (bf16[512,256]{1,0:T(8,128)(2,1)S(1)}, bf16[512,256]{1,0:T(8,128)(2,1)}, u32[]{:S(2)}) copy-start(bf16[512,256]{1,0:T(8,128)(2,1)} %param.11) | copy-start | bytes 786436
  8.6 15.3 %all-to-all-start = ((s32[16,1,1]{2,1,0:T(1,128)}), s32[16,1,1]{2,1,0:T(1,128)S(1)}, u32[]{:S(2)}, u32[]{:S(2)}) async-start(s32[16,1,1]{2,1,0:T(1,128)} %copy.46), calls=%async_computation | async-start | bytes 16384 | tf_op jit(solution)/shard_map/all_to_all | solution.py:48
  26.2 5.1 copy-start.6
  26.2 5.3 copy-start.2
  26.2 5.3 copy-start.4
  26.2 52.3 %all-to-all-start.1 = ((bf16[16,128,512]{2,1,0:T(8,128)(2,1)}), bf16[16,128,512]{2,1,0:T(8,128)(2,1)S(1)}, u32[]{:S(2)}, u32[]{:S(2)}) async-start(bf16[16,128,512]{2,1,0:T(8,128)(2,1)} %gather_fusion), calls=%async_computation.1 | async-start | bytes 4194304 | tf_op jit(solution)/shard_map/all_to_all | solution.py:57
  80.2 1.7 copy-start.1
  149.9 6.9 %copy-start.3 = (bf16[256,256]{1,0:T(8,128)(2,1)S(1)}, bf16[256,256]{1,0:T(8,128)(2,1)}, u32[]{:S(2)}) copy-start(bf16[256,256]{1,0:T(8,128)(2,1)} %param.10) | copy-start | bytes 393220
  149.9 54.2 %all-to-all-start.2 = ((bf16[16,128,512]{1,2,0:T(8,128)(2,1)}), bf16[16,128,512]{1,2,0:T(8,128)(2,1)}, u32[]{:S(2)}, u32[]{:S(2)}) async-start(bf16[16,128,512]{1,2,0:T(8,128)(2,1)} %pad_maximum_fusion), calls=%async_computation.2 | async-start | bytes 4194304 | tf_op jit(solution)/shard_map/all_to_all | solution.py:83
  156.8 331.9 %all-reduce.6.cloned.1.call-start = ((), (), s32[]{:S(2)}) async-start(), calls=%async_computation.4 | async-start | bytes 1572864 | tf_op jit(solution)/shard_map/psum | solution.py:109
  208.0 3.4 copy-start.8
  208.7 3.1 copy-start.9
  211.3 1.8 copy-start.5
  211.3 1.8 copy-start.7
  211.4 437.6 %all-reduce.4.cloned.1.call-start = ((), (), s32[]{:S(2)}) async-start(), calls=%async_computation.3 | async-start | bytes 1048576 | tf_op jit(solution)/shard_map/psum | solution.py:105
Sparse Core Ops, SparseCore 0:
  211.5 277.0 all-reduce.5
  492.0 156.9 all-reduce.3
where the time goes:
time: 659 us; the launch traced here: 657 us
  waiting for transfers between devices  529 us (80%)
  matrix products  48.8 us (7%)
  local copies, waits for them, and re-layouts  38.4 us (6%)
  starting transfers between devices  21.1 us (3%)
  between operations  14.3 us (2%)
    psum x1, waiting for transfers between devices, per_device(): weight_sums = lax.psum((wq_term, wk_term, wv_term), ('grp', 'ops'))  275 us
    psum x1, waiting for transfers between devices, per_device(): summed_total = lax.psum(machine_part, 'ops')  156 us
    all_to_all x1, waiting for transfers between devices, per_device(): lax.all_to_all(outgoing, 'grp', split_axis=0, concat_axis=0, tiled=True)  46.8 us
    all_to_all x1, waiting for transfers between devices, per_device(): lax.all_to_all(jnp.concatenate([key_grads, value_grads], axis=2), 'grp',...  46.3 us
    dot_general x16, matrix products, slot_grads(): jnp.einsum('ohc,mhc->ohm', cotangent4, value_rows, preferred_element_type...  20.9 us
  transfers between devices with their start and end apart: 5, of which 5 were waited for; matrix products, arithmetic and copies ran while one was open for 1% of the time, Pallas kernels for 0%

commit v1 on v0

--- a/solution.py
+++ b/solution.py
@@ -102,7 +102,7 @@
     embed_f = machine_embed.astype(jnp.float32)
     wk_term = jnp.dot(embed_f.T, key_total, precision=highest)
     wv_term = jnp.dot(embed_f.T, value_total, precision=highest)
-    summed_total = lax.psum(machine_part, "ops")
+    summed_total = jnp.sum(lax.all_gather(machine_part, "ops"), axis=0)
     share_rows = machine_rows // lax.axis_size("ops")
     first_row = lax.axis_index("ops") * share_rows
     machine_grad = lax.dynamic_slice_in_dim(summed_total, first_row, share_rows, 0)

time: 659 us -> 569 us (0.86)
  the two profiles are of different devices: /device:TPU:8 before, /device:TPU:17 now
where the time goes in v1:
time: 569 us; the launch traced here: 567 us
  waiting for transfers between devices  430 us (76%)
  matrix products  50.5 us (9%)
  local copies, waits for them, and re-layouts  37.2 us (7%)
  starting transfers between devices  22 us (4%)
  between operations  15.7 us (3%)
  other arithmetic  11.5 us (2%)
    psum x1, waiting for transfers between devices, per_device(): weight_sums = lax.psum((wq_term, wk_term, wv_term), ('grp', 'ops'))  332 us
    all_to_all x1, waiting for transfers between devices, per_device(): lax.all_to_all(outgoing, 'grp', split_axis=0, concat_axis=0, tiled=True)  47.1 us
    all_to_all x1, waiting for transfers between devices, per_device(): lax.all_to_all(jnp.concatenate([key_grads, value_grads], axis=2), 'grp',...  46.5 us
    dot_general x16, matrix products, slot_grads(): jnp.einsum('ohc,mhc->ohm', cotangent4, value_rows, preferred_element_type...  20.9 us
  transfers between devices with their start and end apart: 5, of which 4 were waited for; matrix products, arithmetic and copies ran while one was open for 2% of the time, Pallas kernels for 0%

profile of v1, /device:TPU:17, one launch (start us, length us, event | category | flops | bytes accessed | tf_op | source)
XLA Modules:
  0.0 567.1 jit_solution(2654259179481988658)
XLA Ops:
  8.0 1.4 copy.46
  9.4 9.2 %all-to-all-start = ((s32[16,1,1]{2,1,0:T(1,128)}), s32[16,1,1]{2,1,0:T(1,128)S(1)}, u32[]{:S(2)}, u32[]{:S(2)}) async-start(s32[16,1,1]{2,1,0:T(1,128)} %copy.46), calls=%async_computation | async-start | bytes 16384 | tf_op jit(solution)/shard_map/all_to_all | solution.py:48
  18.6 1.3 convolution_convert_fusion.1
  19.9 3.7 all-to-all-done
  24.1 2.0 gather_fusion
  26.1 6.3 %all-to-all-start.1 = ((bf16[16,128,512]{2,1,0:T(8,128)(2,1)}), bf16[16,128,512]{2,1,0:T(8,128)(2,1)S(1)}, u32[]{:S(2)}, u32[]{:S(2)}) async-start(bf16[16,128,512]{2,1,0:T(8,128)(2,1)} %gather_fusion), calls=%async_computation.1 | async-start | bytes 4194304 | tf_op jit(solution)/shard_map/all_to_all | solution.py:57
  32.8 47.1 %all-to-all-done.1 = bf16[16,128,512]{2,1,0:T(8,128)(2,1)S(1)} async-done(((bf16[16,128,512]{2,1,0:T(8,128)(2,1)}), bf16[16,128,512]{2,1,0:T(8,128)(2,1)S(1)}, u32[]{:S(2)}, u32[]{:S(2)}) %all-to-all-start.1) | async-done | bytes 2097184 | tf_op jit(solution)/shard_map/all_to_all | solution.py:57
  79.9 1.6 fusion.38
  81.5 1.7 copy.47
  83.2 1.3 copy.48
  84.5 63.7 %while.15 = (s32[]{:T(128)}, f32[256,8,32]{0,2,1:T(8,128)S(1)}, bf16[16,128,256]{1,2,0:T(8,128)(2,1)}, bf16[16,128,256]{1,2,0:T(8,128)(2,1)}, bf16[16,128,8,32]{...) while((s32[]{:T(128)}, f32[256,8,32]{0,2,1:T(8,128)S(1)}, ...), condition=%wide.region_1.2_spmd.clone, body=%wide.region_0.1_spmd.clone.sunk | while | flops 87785472 | bytes 6362243 | solution.py:74
  85.0 0.7 constant_dynamic-slice_fusion.3
  85.7 1.3 fusion.80
  87.6 0.7 bitcast_dynamic-update-slice_fusion.3
  89.0 0.7 constant_dynamic-slice_fusion.3
  89.7 1.3 fusion.80
  93.0 0.7 constant_dynamic-slice_fusion.3
  93.7 1.3 fusion.80
  97.0 0.7 constant_dynamic-slice_fusion.3
  97.7 1.3 fusion.80
  101.0 0.7 constant_dynamic-slice_fusion.3
  101.7 1.3 fusion.80
  104.9 0.7 constant_dynamic-slice_fusion.3
  105.6 1.3 fusion.80
  108.9 0.7 constant_dynamic-slice_fusion.3
  109.6 1.3 fusion.80
  111.5 0.7 bitcast_dynamic-update-slice_fusion.3
  112.9 0.7 constant_dynamic-slice_fusion.3
  113.6 1.3 fusion.80
  116.9 0.7 constant_dynamic-slice_fusion.3
  117.6 1.3 fusion.80
  120.8 0.7 constant_dynamic-slice_fusion.3
  121.6 1.3 fusion.80
  124.8 0.7 constant_dynamic-slice_fusion.3
  125.5 1.3 fusion.80
  128.8 0.7 constant_dynamic-slice_fusion.3
  129.5 1.3 fusion.80
  131.4 0.7 bitcast_dynamic-update-slice_fusion.3
  132.8 0.7 constant_dynamic-slice_fusion.3
  133.5 1.3 fusion.80
  135.4 0.7 bitcast_dynamic-update-slice_fusion.3
  136.8 0.7 constant_dynamic-slice_fusion.3
  137.5 1.3 fusion.80
  140.8 0.7 constant_dynamic-slice_fusion.3
  141.5 1.3 fusion.80
  144.7 0.7 constant_dynamic-slice_fusion.3
  145.4 1.3 fusion.80
  148.2 3.1 pad_maximum_fusion
  151.3 6.4 %all-to-all-start.2 = ((bf16[16,128,512]{1,2,0:T(8,128)(2,1)}), bf16[16,128,512]{1,2,0:T(8,128)(2,1)S(1)}, u32[]{:S(2)}, u32[]{:S(2)}) async-start(bf16[16,128,512]{1,2,0:T(8,128)(2,1)} %pad_maximum_fusion), calls=%async_computation.2 | async-start | bytes 4194304 | tf_op jit(solution)/shard_map/all_to_all | solution.py:83
  157.8 0.9 convolution_bitcast_fusion.3
  158.7 46.5 %all-to-all-done.2 = bf16[16,128,512]{1,2,0:T(8,128)(2,1)S(1)} async-done(((bf16[16,128,512]{1,2,0:T(8,128)(2,1)}), bf16[16,128,512]{1,2,0:T(8,128)(2,1)S(1)}, u32[]{:S(2)}, u32[]{:S(2)}) %all-to-all-start.2) | async-done | bytes 2097184 | tf_op jit(solution)/shard_map/all_to_all | solution.py:83
  205.2 3.0 copy.57
  208.2 2.2 fusion.34
  210.4 0.7 reshape.79
  211.1 1.3 convolution_bitcast_fusion.1
  212.4 1.3 convolution_bitcast_fusion.2
  214.2 1.2 convolution_add_fusion
  215.5 0.9 fusion.25
  216.3 332.2 %all-reduce.3.cloned.1.call-done = (f32[256,256]{0,1:T(8,128)}, f32[256,256]{0,1:T(8,128)}, f32[256,256]{0,1:T(8,128)}) async-done(((f32[256,256]{0,1:T(8,128)}, f32[256,256]{0,1:T(8,128)}, f32[256,256]{0,1:T(8,128)}), (f32[256,256]{0,1:T(8,128)}, f32[256,256]{0,1:T(8,128)}, f32[256,256]{0,1:T(8,128)})) %all-reduce.3.cloned.1.call-update) | async-done | bytes 786448 | tf_op jit(solution)/shard_map/psum | solution.py:109
  548.5 1.1 broadcast_multiply_fusion
  549.6 0.8 copy.52
  550.4 0.8 copy.53
  551.3 0.8 copy.51
  552.2 6.9 %reduce_sum.9 = f32[512,256]{1,0:T(8,128)S(1)} reduce(f32[32,512,256]{2,1,0:T(8,128)} %bitcast.106, f32[]{:T(128)} %constant.16.clone.1), dimensions={0}, to_apply=%region_2.3 | reduce | flops 4063232 | bytes 17301508 | tf_op jit(solution)/shard_map/reduce_sum | solution.py:105
  (109 shorter events, 30.1 us)
Async XLA Ops:
  8.0 10.6 %copy-start = (bf16[512,256]{1,0:T(8,128)(2,1)S(1)}, bf16[512,256]{1,0:T(8,128)(2,1)}, u32[]{:S(2)}) copy-start(bf16[512,256]{1,0:T(8,128)(2,1)} %param.11) | copy-start | bytes 786436
  9.4 14.3 %all-to-all-start = ((s32[16,1,1]{2,1,0:T(1,128)}), s32[16,1,1]{2,1,0:T(1,128)S(1)}, u32[]{:S(2)}, u32[]{:S(2)}) async-start(s32[16,1,1]{2,1,0:T(1,128)} %copy.46), calls=%async_computation | async-start | bytes 16384 | tf_op jit(solution)/shard_map/all_to_all | solution.py:48
  26.1 6.3 %copy-start.4 = (bf16[256,256]{1,0:T(8,128)(2,1)S(1)}, bf16[256,256]{1,0:T(8,128)(2,1)}, u32[]{:S(2)}) copy-start(bf16[256,256]{1,0:T(8,128)(2,1)} %param.12) | copy-start | bytes 393220
  26.1 6.4 %copy-start.2 = (bf16[256,256]{1,0:T(8,128)(2,1)S(1)}, bf16[256,256]{1,0:T(8,128)(2,1)}, u32[]{:S(2)}) copy-start(bf16[256,256]{1,0:T(8,128)(2,1)} %param.10) | copy-start | bytes 393220
  26.1 6.4 %copy-start.3 = (bf16[256,256]{1,0:T(8,128)(2,1)S(1)}, bf16[256,256]{1,0:T(8,128)(2,1)}, u32[]{:S(2)}) copy-start(bf16[256,256]{1,0:T(8,128)(2,1)} %param.13) | copy-start | bytes 393220
  26.1 53.8 %all-to-all-start.1 = ((bf16[16,128,512]{2,1,0:T(8,128)(2,1)}), bf16[16,128,512]{2,1,0:T(8,128)(2,1)S(1)}, u32[]{:S(2)}, u32[]{:S(2)}) async-start(bf16[16,128,512]{2,1,0:T(8,128)(2,1)} %gather_fusion), calls=%async_computation.1 | async-start | bytes 4194304 | tf_op jit(solution)/shard_map/all_to_all | solution.py:57
  81.5 1.7 copy-start.1
  151.3 53.9 %all-to-all-start.2 = ((bf16[16,128,512]{1,2,0:T(8,128)(2,1)}), bf16[16,128,512]{1,2,0:T(8,128)(2,1)S(1)}, u32[]{:S(2)}, u32[]{:S(2)}) async-start(bf16[16,128,512]{1,2,0:T(8,128)(2,1)} %pad_maximum_fusion), calls=%async_computation.2 | async-start | bytes 4194304 | tf_op jit(solution)/shard_map/all_to_all | solution.py:83
  157.7 390.8 %all-reduce.3.cloned.1.call-start = ((), (), s32[]{:S(2)}) async-start(), calls=%async_computation.4 | async-start | bytes 1572864 | tf_op jit(solution)/shard_map/psum | solution.py:109
  210.3 3.4 copy-start.5
  211.1 3.1 copy-start.6
  213.7 338.4 %all-gather.3.cloned.1.call-start = ((), (), s32[]{:S(2)}) async-start(), calls=%async_computation.3 | async-start | bytes 17301504 | tf_op jit(solution)/shard_map/all_gather | solution.py:105
  548.5 2.8 copy-start.7
Sparse Core Ops, SparseCore 0:
  213.8 334.6 all-reduce.2
Sparse Core Ops, SparseCore 1:
  217.4 147.3 all-gather.2
